TPU v7x, 256 devices: a whole 4x4x8 slice. The times are simulated.
256 devices in a mesh: section: 16 (over z_lo, y), tensor: 16 (over x, z_hi, core).
Axes of the slice: x: 4, y: 4, z: 8 (z_hi: 2, z_lo: 4; z = z_hi * 4 + z_lo), core: 2. Of those that a mesh axis runs over, the one named last changes fastest.
Arguments:
- inputs_down: bfloat16 [16, 224, 8192], P('section', None, 'tensor'), may hold values from -18 to 18
- inputs_up: bfloat16 [16, 224, 8192], P('section', None, 'tensor'), may hold values from -18 to 18
- grads_down: bfloat16 [16, 224, 8192], P('section', None, 'tensor'), may hold values from -6 to 6
- grads_up: bfloat16 [16, 224, 8192], P('section', None, 'tensor'), may hold values from -6 to 6
- weights_down: bfloat16 [16, 8192, 2048], P('section', 'tensor'), may hold values from -0.5 to 0.5
- weights_up: bfloat16 [16, 8192, 2048], P('section', 'tensor'), may hold values from -0.5 to 0.5
Outputs:
- handed_down: bfloat16 [16, 224, 8192], P('section', None, 'tensor')
- handed_up: bfloat16 [16, 224, 8192], P('section', None, 'tensor')
- returned_down: bfloat16 [16, 224, 8192], P('section', None, 'tensor')
- returned_up: bfloat16 [16, 224, 8192], P('section', None, 'tensor')
- weight_grads: float32 [16, 8192, 2048], P('section', 'tensor')
All inputs are finite; a program needn't handle non-finite values.
Results may differ from a plain program's by a relative error of at most 0.0095.
Values may be sent and summed in bfloat16 or wider, within the bound.
A program may use at most 64 MiB of HBM per device.

v0:
```python
import jax
import jax.numpy as jnp
from jax import lax
from jax.sharding import PartitionSpec as P

D = 8192
HEADS = 64
KV_HEADS = 8
HEAD_DIM = 128
EPS = 1e-05
NEG_BIG = -1e30


def cut_along(x, dim, count):
    before, after = (x.shape[:dim], x.shape[dim + 1 :])
    return jnp.moveaxis(x.reshape(*before, count, -1, *after), dim, 0)


def sum_at_owner(x, axis, dim):
    count = lax.axis_size(axis)
    tiles = lax.all_to_all(cut_along(x, dim, count), axis, 0, 0, tiled=True)
    return jnp.sum(tiles, axis=0)


def shortened(x):

    def short(part):
        return part.astype(jnp.bfloat16) if part.dtype == jnp.float32 else part

    return jax.tree.map(short, x)


def copy_for_each(x, axis):
    count = lax.axis_size(axis)
    return lax.all_to_all(jnp.broadcast_to(x[None], (count, *x.shape)), axis, 0, 0, tiled=True)


def taken_together(x, axis):
    return copy_for_each(x, axis).sum(axis=0)


def passed_along(x, axis, by):
    count = lax.axis_size(axis)
    pairs = [(i, i + by) for i in range(count) if 0 <= i + by < count]
    return lax.ppermute(x, axis, pairs)


def combine_tensor(partial_value):
    share = sum_at_owner(partial_value, "tensor", 1).astype(jnp.bfloat16)
    return lax.all_gather(share, "tensor", axis=1, tiled=True)


def reflect_blocks(parts):
    flipped = tuple((jnp.flip(piece, 1) for piece in parts))
    return jax.tree.map(
        lambda part, own: part.astype(own.dtype),
        lax.all_to_all(shortened(flipped), "section", split_axis=1, concat_axis=1, tiled=True),
        flipped,
    )


def mirror_terms(payload):
    sections = lax.axis_size("section")
    split = tuple(
        (piece.reshape(piece.shape[0], sections, piece.shape[1] // sections) for piece in payload)
    )
    moved = reflect_blocks(
        (
            lax.all_to_all(split[0], "section", split_axis=1, concat_axis=1, tiled=True),
            lax.all_to_all(split[1], "section", split_axis=1, concat_axis=1, tiled=True),
        )
    )
    return tuple(
        (piece.reshape(piece.shape[0], piece.shape[1] * piece.shape[2]) for piece in moved)
    )


def section_pass(inputs, grads, weights):
    tokens, width_here = inputs.shape
    heads_here = width_here // HEAD_DIM
    kv_width = weights.shape[1] // 2
    scale = HEAD_DIM ** (-0.5)
    x_float = inputs.astype(jnp.float32)
    squares = taken_together(jnp.sum(x_float * x_float, axis=1), "tensor")
    scale_rows = lax.rsqrt(squares / D + EPS)[:, None]
    normed = x_float * scale_rows
    hidden = normed.astype(jnp.bfloat16)
    keyval = combine_tensor(jnp.dot(hidden, weights, preferred_element_type=jnp.float32))
    head_ids = lax.axis_index("tensor") * heads_here + jnp.arange(heads_here)
    selector = (head_ids[:, None] // (HEADS // KV_HEADS) == jnp.arange(KV_HEADS)[None, :]).astype(
        jnp.float32
    )
    keys_all = keyval[:, :kv_width].reshape(tokens, KV_HEADS, HEAD_DIM).astype(jnp.float32)
    values_all = keyval[:, kv_width:].reshape(tokens, KV_HEADS, HEAD_DIM).astype(jnp.float32)
    key_rows = jnp.einsum("hj,ljd->lhd", selector, keys_all)
    value_rows = jnp.einsum("hj,ljd->lhd", selector, values_all)
    queries = hidden.reshape(tokens, heads_here, HEAD_DIM).astype(jnp.float32)
    places = jnp.arange(tokens)
    causal = places[:, None] >= places[None, :]
    scores = jnp.einsum("qhd,khd->hqk", queries, key_rows) * scale
    scores = jnp.where(causal[None], scores, NEG_BIG)
    score_peak = jnp.max(scores, axis=-1, keepdims=True)
    score_exp = jnp.exp(scores - score_peak)
    attn_probs = score_exp / jnp.sum(score_exp, axis=-1, keepdims=True)
    probs_low = lax.optimization_barrier(attn_probs.astype(jnp.bfloat16)).astype(jnp.float32)
    attended = jnp.einsum("hqk,khd->qhd", probs_low, value_rows).reshape(tokens, width_here)
    output = (x_float + attended).astype(jnp.bfloat16)
    upstream = grads.astype(jnp.float32).reshape(tokens, heads_here, HEAD_DIM)
    grad_prob = jnp.einsum("qhd,khd->hqk", upstream, value_rows)
    grad_value_heads = jnp.einsum("hqk,qhd->khd", probs_low, upstream)
    grad_score = attn_probs * (grad_prob - jnp.sum(attn_probs * grad_prob, axis=-1, keepdims=True))
    grad_score_low = lax.optimization_barrier(grad_score.astype(jnp.bfloat16)).astype(jnp.float32)
    grad_query = jnp.einsum("hqk,khd->qhd", grad_score_low, key_rows) * scale
    grad_key_heads = jnp.einsum("hqk,qhd->khd", grad_score_low, queries) * scale
    grad_keys = jnp.einsum("hj,lhd->ljd", selector, grad_key_heads).reshape(tokens, kv_width)
    grad_values = jnp.einsum("hj,lhd->ljd", selector, grad_value_heads).reshape(tokens, kv_width)
    grad_kv = combine_tensor(jnp.concatenate([grad_keys, grad_values], axis=1))
    grad_hidden = grad_query.reshape(tokens, width_here) + jnp.dot(
        grad_kv, weights.T, preferred_element_type=jnp.float32
    )
    inner_sum = taken_together(jnp.sum(grad_hidden * normed, axis=1), "tensor")
    grad_input = (
        grads.astype(jnp.float32) + scale_rows * (grad_hidden - normed * (inner_sum / D)[:, None])
    ).astype(jnp.bfloat16)
    grad_weights = jnp.dot(hidden.T, grad_kv, preferred_element_type=jnp.float32)
    return (output, grad_input, grad_weights, hidden, grad_kv)


def on_device(inputs_down, inputs_up, grads_down, grads_up, weights_down, weights_up):
    out_down, back_down, dw_down, hidden_down, gkv_down = section_pass(
        inputs_down[0], grads_down[0], weights_down[0]
    )
    handed_down = passed_along(out_down, "section", 1)
    out_up, back_up, dw_up, hidden_up, gkv_up = section_pass(
        inputs_up[0], grads_up[0], weights_up[0]
    )
    handed_up = passed_along(out_up, "section", -1)
    returned_down = passed_along(back_down, "section", -1)
    returned_up = passed_along(back_up, "section", 1)
    carried_hidden, carried_kv = mirror_terms((hidden_up, gkv_up))
    weight_grads = dw_down + jnp.dot(
        carried_hidden.T, carried_kv, preferred_element_type=jnp.float32
    )
    return (
        handed_down[None],
        handed_up[None],
        returned_down[None],
        returned_up[None],
        weight_grads[None],
    )


def solution(mesh):
    in_specs = (
        P("section", None, "tensor"),
        P("section", None, "tensor"),
        P("section", None, "tensor"),
        P("section", None, "tensor"),
        P("section", "tensor", None),
        P("section", "tensor", None),
    )
    out_specs = (
        P("section", None, "tensor"),
        P("section", None, "tensor"),
        P("section", None, "tensor"),
        P("section", None, "tensor"),
        P("section", "tensor", None),
    )
    return jax.shard_map(
        on_device, mesh=mesh, in_specs=in_specs, out_specs=out_specs, check_vma=False
    )
```

profile of v0, /device:TPU:64, one launch (start us, length us, event | category | flops | bytes accessed | tf_op | source)
XLA Modules:
  0.0 522.0 jit_solution(3485464926994449465)
XLA Ops:
  2.5 9.2 %all-to-all-start.2 = ((f32[16,1,224]{2,1,0:T(1,128)}), f32[16,1,224]{2,1,0:T(1,128)S(1)}, u32[]{:S(2)}, u32[]{:S(2)}) async-start(f32[16,1,224]{2,1,0:T(1,128)} %broadcast_in_dim.40), calls=%async_computation.2 | async-start | bytes 32768 | tf_op jit(solution)/shard_map/all_to_all | solution.py:35
  13.9 7.8 %all-to-all-done.2 = f32[16,1,224]{2,1,0:T(1,128)S(1)} async-done(((f32[16,1,224]{2,1,0:T(1,128)}), f32[16,1,224]{2,1,0:T(1,128)S(1)}, u32[]{:S(2)}, u32[]{:S(2)}) %all-to-all-start.2) | async-done | bytes 14368 | tf_op jit(solution)/shard_map/all_to_all | solution.py:35
  22.3 3.5 all-to-all-start
  26.6 9.1 %all-to-all-done = f32[16,1,224]{2,1,0:T(1,128)S(1)} async-done(((f32[16,1,224]{2,1,0:T(1,128)}), f32[16,1,224]{2,1,0:T(1,128)S(1)}, u32[]{:S(2)}, u32[]{:S(2)}) %all-to-all-start) | async-done | bytes 14368 | tf_op jit(solution)/shard_map/all_to_all | solution.py:35
  35.8 7.3 %all-to-all-start.8 = ((bf16[224,16,32]{0,2,1:T(8,128)(2,1)}), bf16[224,16,32]{0,2,1:T(8,128)(2,1)S(1)}, u32[]{:S(2)}, u32[]{:S(2)}) async-start(bf16[224,16,32]{0,2,1:T(8,128)(2,1)} %multiply_convert_fusion), calls=%async_computation.8 | async-start | bytes 524288 | tf_op jit(solution)/shard_map/all_to_all | solution.py:69
  43.1 2.5 copy.195
  45.6 3.6 convolution_bitcast_fusion
  49.2 3.0 all-to-all-done.8
  52.2 4.4 all-to-all-start.3
  56.7 4.0 copy.194
  60.7 3.6 convolution_bitcast_fusion.1
  64.3 40.8 %all-to-all-done.3 = f32[16,224,128]{2,1,0:T(8,128)} async-done(((f32[16,224,128]{2,1,0:T(8,128)}), f32[16,224,128]{2,1,0:T(8,128)}, u32[]{:S(2)}, u32[]{:S(2)}) %all-to-all-start.3) | async-done | bytes 1835040 | tf_op jit(solution)/shard_map/all_to_all | solution.py:21
  105.1 4.4 all-to-all-start.1
  113.3 1.6 reduce_sum.150
  114.8 60.1 %all_gather.13 = bf16[224,2048]{1,0:T(8,128)(2,1)S(1)} all-gather(bf16[224,128]{1,0:T(8,128)(2,1)S(1)} %reduce_sum.150), channel_id=1, replica_groups=mesh['section'=16,'tensor'=16] {'tensor'}, dimensions={1}, use_global_device_ids=true | all-gather | bytes 974848 | tf_op jit(solution)/shard_map/all_gather | solution.py:50
  176.3 2.6 fusion.108
  184.2 13.6 %all-to-all-start.9 = ((bf16[224,16,32]{0,2,1:T(8,128)(2,1)}), bf16[224,16,32]{0,2,1:T(8,128)(2,1)S(1)}, u32[]{:S(2)}, u32[]{:S(2)}) async-start(bf16[224,16,32]{0,2,1:T(8,128)(2,1)} %rev.8), calls=%async_computation.9 | async-start | bytes 524288 | tf_op jit(solution)/shard_map/all_to_all | solution.py:57
  199.7 1.8 copy.185
  201.5 1.6 reduce_sum.146
  203.1 4.2 all-to-all-done.9
  207.2 8.9 %all-to-all-start.6 = ((f32[16,224,128]{2,1,0:T(8,128)}), f32[16,224,128]{2,1,0:T(8,128)}, u32[]{:S(2)}, u32[]{:S(2)}) async-start(f32[16,224,128]{2,1,0:T(8,128)} %copy.185), calls=%async_computation.6 | async-start | bytes 3670016 | tf_op jit(solution)/shard_map/all_to_all | solution.py:21
  216.1 72.7 %all_gather.12 = bf16[224,2048]{1,0:T(8,128)(2,1)S(1)} all-gather(bf16[224,128]{1,0:T(8,128)(2,1)S(1)} %reduce_sum.146), channel_id=1, replica_groups=mesh['section'=16,'tensor'=16] {'tensor'}, dimensions={1}, use_global_device_ids=true | all-gather | bytes 974848 | tf_op jit(solution)/shard_map/all_gather | solution.py:50
  290.2 2.6 fusion.105
  297.1 1.8 copy.175
  298.9 9.7 %all-to-all-start.4 = ((f32[16,224,128]{2,1,0:T(8,128)}), f32[16,224,128]{2,1,0:T(8,128)}, u32[]{:S(2)}, u32[]{:S(2)}) async-start(f32[16,224,128]{2,1,0:T(8,128)} %copy.175), calls=%async_computation.4 | async-start | bytes 3670016 | tf_op jit(solution)/shard_map/all_to_all | solution.py:21
  309.7 1.6 reduce_sum.157
  311.3 71.0 %all_gather.15 = bf16[224,2048]{1,0:T(8,128)(2,1)S(1)} all-gather(bf16[224,128]{1,0:T(8,128)(2,1)S(1)} %reduce_sum.157), channel_id=1, replica_groups=mesh['section'=16,'tensor'=16] {'tensor'}, dimensions={1}, use_global_device_ids=true | all-gather | bytes 974848 | tf_op jit(solution)/shard_map/all_gather | solution.py:50
  382.3 2.6 fusion.48
  385.5 8.5 %all-to-all-start.7 = ((f32[16,1,224]{2,1,0:T(1,128)}), f32[16,1,224]{2,1,0:T(1,128)S(1)}, u32[]{:S(2)}, u32[]{:S(2)}) async-start(f32[16,1,224]{2,1,0:T(1,128)} %broadcast_in_dim.44), calls=%async_computation.7 | async-start | bytes 32768 | tf_op jit(solution)/shard_map/all_to_all | solution.py:35
  395.2 8.9 %all-to-all-done.7 = f32[16,1,224]{2,1,0:T(1,128)S(1)} async-done(((f32[16,1,224]{2,1,0:T(1,128)}), f32[16,1,224]{2,1,0:T(1,128)S(1)}, u32[]{:S(2)}, u32[]{:S(2)}) %all-to-all-start.7) | async-done | bytes 14368 | tf_op jit(solution)/shard_map/all_to_all | solution.py:35
  404.1 4.4 all-to-all-start.10
  408.5 2.4 fusion.27
  412.5 36.8 %all_gather.14 = bf16[224,2048]{1,0:T(8,128)(2,1)S(1)} all-gather(bf16[224,128]{1,0:T(8,128)(2,1)S(1)} %reduce_sum.153), channel_id=1, replica_groups=mesh['section'=16,'tensor'=16] {'tensor'}, dimensions={1}, use_global_device_ids=true | all-gather | bytes 974848 | tf_op jit(solution)/shard_map/all_gather | solution.py:50
  449.3 2.6 fusion.55
  452.6 8.0 %all-to-all-start.5 = ((f32[16,1,224]{2,1,0:T(1,128)}), f32[16,1,224]{2,1,0:T(1,128)S(1)}, u32[]{:S(2)}, u32[]{:S(2)}) async-start(f32[16,1,224]{2,1,0:T(1,128)} %broadcast_in_dim.42), calls=%async_computation.5 | async-start | bytes 32768 | tf_op jit(solution)/shard_map/all_to_all | solution.py:35
  460.6 2.3 rev.9
  462.8 7.7 %all-to-all-done.5 = f32[16,1,224]{2,1,0:T(1,128)S(1)} async-done(((f32[16,1,224]{2,1,0:T(1,128)}), f32[16,1,224]{2,1,0:T(1,128)S(1)}, u32[]{:S(2)}, u32[]{:S(2)}) %all-to-all-start.5) | async-done | bytes 14368 | tf_op jit(solution)/shard_map/all_to_all | solution.py:35
  470.6 9.9 %all-to-all-start.11 = ((bf16[224,16,128]{2,0,1:T(8,128)(2,1)}), bf16[224,16,128]{2,0,1:T(8,128)(2,1)S(1)}, u32[]{:S(2)}, u32[]{:S(2)}) async-start(bf16[224,16,128]{2,0,1:T(8,128)(2,1)} %rev.9), calls=%async_computation.11 | async-start | bytes 1835008 | tf_op jit(solution)/shard_map/all_to_all | solution.py:57
  483.0 2.3 fusion.36
  485.3 3.4 collective-permute-start.3
  488.6 4.6 collective-permute-start.1
  493.5 2.5 collective-permute-start.2
  496.0 3.5 collective-permute-start
  499.5 2.8 fusion.69
  502.3 6.8 %collective-permute-done.3 = bf16[224,512]{1,0:T(8,128)(2,1)S(1)} collective-permute-done((bf16[224,512]{1,0:T(8,128)(2,1)}, bf16[224,512]{1,0:T(8,128)(2,1)S(1)}, u32[]{:S(2)}, u32[]{:S(2)}) %collective-permute-start.3) | collective-permute-done | bytes 229408 | tf_op jit(solution)/shard_map/ppermute | solution.py:45
  510.1 3.2 collective-permute-done
  513.4 4.9 add_bitcast_fusion
  519.0 1.6 copy.280
  (119 shorter events, 34.1 us)
Async XLA Ops:
  0.6 42.4 %copy-start.1 = (bf16[1,512,2048]{2,1,0:T(8,128)(2,1)S(1)}, bf16[1,512,2048]{2,1,0:T(8,128)(2,1)}, u32[]{:S(2)}) copy-start(bf16[1,512,2048]{2,1,0:T(8,128)(2,1)} %param.11) | copy-start | bytes 6291460
  2.5 19.2 %all-to-all-start.2 = ((f32[16,1,224]{2,1,0:T(1,128)}), f32[16,1,224]{2,1,0:T(1,128)S(1)}, u32[]{:S(2)}, u32[]{:S(2)}) async-start(f32[16,1,224]{2,1,0:T(1,128)} %broadcast_in_dim.40), calls=%async_computation.2 | async-start | bytes 32768 | tf_op jit(solution)/shard_map/all_to_all | solution.py:35
  22.3 13.4 %all-to-all-start = ((f32[16,1,224]{2,1,0:T(1,128)}), f32[16,1,224]{2,1,0:T(1,128)S(1)}, u32[]{:S(2)}, u32[]{:S(2)}) async-start(f32[16,1,224]{2,1,0:T(1,128)} %broadcast_in_dim.36), calls=%async_computation | async-start | bytes 32768 | tf_op jit(solution)/shard_map/all_to_all | solution.py:35
  35.8 16.5 %all-to-all-start.8 = ((bf16[224,16,32]{0,2,1:T(8,128)(2,1)}), bf16[224,16,32]{0,2,1:T(8,128)(2,1)S(1)}, u32[]{:S(2)}, u32[]{:S(2)}) async-start(bf16[224,16,32]{0,2,1:T(8,128)(2,1)} %multiply_convert_fusion), calls=%async_computation.8 | async-start | bytes 524288 | tf_op jit(solution)/shard_map/all_to_all | solution.py:69
  43.1 2.5 copy-start.3
  52.2 52.9 %all-to-all-start.3 = ((f32[16,224,128]{2,1,0:T(8,128)}), f32[16,224,128]{2,1,0:T(8,128)}, u32[]{:S(2)}, u32[]{:S(2)}) async-start(f32[16,224,128]{2,1,0:T(8,128)} %convolution_bitcast_fusion), calls=%async_computation.3 | async-start | bytes 3670016 | tf_op jit(solution)/shard_map/all_to_all | solution.py:21
  56.7 4.0 copy-start
  64.3 47.1 %copy-start.22 = (bf16[1,224,512]{2,1,0:T(8,128)(2,1)S(1)}, bf16[1,224,512]{2,1,0:T(8,128)(2,1)}, u32[]{:S(2)}) copy-start(bf16[1,224,512]{2,1,0:T(8,128)(2,1)} %param.8) | copy-start | bytes 688132
  105.1 79.1 %all-to-all-start.1 = ((f32[16,224,128]{2,1,0:T(8,128)}), f32[16,224,128]{2,1,0:T(8,128)}, u32[]{:S(2)}, u32[]{:S(2)}) async-start(f32[16,224,128]{2,1,0:T(8,128)} %convolution_bitcast_fusion.1), calls=%async_computation.1 | async-start | bytes 3670016 | tf_op jit(solution)/shard_map/all_to_all | solution.py:21
  176.2 3.9 copy-start.24
  178.8 3.2 copy-start.21
  180.2 2.1 copy-start.4
  181.7 0.7 copy-start.8
  182.0 1.2 copy-start.16
  182.4 0.8 copy-start.11
  184.2 23.0 %all-to-all-start.9 = ((bf16[224,16,32]{0,2,1:T(8,128)(2,1)}), bf16[224,16,32]{0,2,1:T(8,128)(2,1)S(1)}, u32[]{:S(2)}, u32[]{:S(2)}) async-start(bf16[224,16,32]{0,2,1:T(8,128)(2,1)} %rev.8), calls=%async_computation.9 | async-start | bytes 524288 | tf_op jit(solution)/shard_map/all_to_all | solution.py:57
  207.2 8.9 %copy-start.18 = (bf16[224,16,32]{0,2,1:T(8,128)(2,1)}, bf16[224,16,32]{0,2,1:T(8,128)(2,1)S(1)}, u32[]{:S(2)}) copy-start(bf16[224,16,32]{0,2,1:T(8,128)(2,1)S(1)} %all-to-all-done.9) | copy-start | bytes 688132
  207.2 91.7 %all-to-all-start.6 = ((f32[16,224,128]{2,1,0:T(8,128)}), f32[16,224,128]{2,1,0:T(8,128)}, u32[]{:S(2)}, u32[]{:S(2)}) async-start(f32[16,224,128]{2,1,0:T(8,128)} %copy.185), calls=%async_computation.6 | async-start | bytes 3670016 | tf_op jit(solution)/shard_map/all_to_all | solution.py:21
  289.8 4.3 copy-start.14
  290.2 3.9 copy-start.26
  292.7 2.0 copy-start.20
  294.1 1.0 copy-start.6
  294.5 0.7 copy-start.10
  294.8 1.0 copy-start.15
  295.1 1.8 copy-start.13
  298.9 9.7 %copy-start.12 = (bf16[4,224,224]{1,2,0:T(8,128)(2,1)S(1)}, bf16[4,224,224]{1,2,0:T(8,128)(2,1)}, u32[]{:S(2)}) copy-start(bf16[4,224,224]{1,2,0:T(8,128)(2,1)} %copy-done.11) | copy-start | bytes 1204228
  298.9 9.7 %copy-start.25 = (bf16[224,4,128]{2,1,0:T(4,128)(2,1)S(1)}, bf16[224,4,128]{2,1,0:T(4,128)(2,1)}, u32[]{:S(2)}) copy-start(bf16[224,4,128]{2,1,0:T(4,128)(2,1)} %copy-done.24) | copy-start | bytes 688132
  298.9 86.0 %all-to-all-start.4 = ((f32[16,224,128]{2,1,0:T(8,128)}), f32[16,224,128]{2,1,0:T(8,128)}, u32[]{:S(2)}, u32[]{:S(2)}) async-start(f32[16,224,128]{2,1,0:T(8,128)} %copy.175), calls=%async_computation.4 | async-start | bytes 3670016 | tf_op jit(solution)/shard_map/all_to_all | solution.py:21
  385.5 18.5 %all-to-all-start.7 = ((f32[16,1,224]{2,1,0:T(1,128)}), f32[16,1,224]{2,1,0:T(1,128)S(1)}, u32[]{:S(2)}, u32[]{:S(2)}) async-start(f32[16,1,224]{2,1,0:T(1,128)} %broadcast_in_dim.44), calls=%async_computation.7 | async-start | bytes 32768 | tf_op jit(solution)/shard_map/all_to_all | solution.py:35
  404.1 47.9 %all-to-all-start.10 = ((bf16[224,16,128]{2,0,1:T(8,128)(2,1)}), bf16[224,16,128]{2,0,1:T(8,128)(2,1)}, u32[]{:S(2)}, u32[]{:S(2)}) async-start(bf16[224,16,128]{2,0,1:T(8,128)(2,1)} %copy_bitcast_fusion), calls=%async_computation.10 | async-start | bytes 1835008 | tf_op jit(solution)/shard_map/all_to_all | solution.py:70
  408.5 40.8 %copy-start.2 = (bf16[1,512,2048]{2,1,0:T(8,128)(2,1)S(1)}, bf16[1,512,2048]{2,1,0:T(8,128)(2,1)}, u32[]{:S(2)}) copy-start(bf16[1,512,2048]{2,1,0:T(8,128)(2,1)} %param.10) | copy-start | bytes 6291460
  452.0 28.5 %copy-start.5 = (bf16[4,224,224]{1,2,0:T(8,128)(2,1)S(1)}, bf16[4,224,224]{1,2,0:T(8,128)(2,1)}, u32[]{:S(2)}) copy-start(bf16[4,224,224]{1,2,0:T(8,128)(2,1)} %copy-done.4) | copy-start | bytes 1204228
  452.0 28.5 %copy-start.9 = (bf16[224,4,128]{2,1,0:T(4,128)(2,1)S(1)}, bf16[224,4,128]{2,1,0:T(4,128)(2,1)}, u32[]{:S(2)}) copy-start(bf16[224,4,128]{2,1,0:T(4,128)(2,1)} %copy-done.8) | copy-start | bytes 688132
  452.6 18.0 %all-to-all-start.5 = ((f32[16,1,224]{2,1,0:T(1,128)}), f32[16,1,224]{2,1,0:T(1,128)S(1)}, u32[]{:S(2)}, u32[]{:S(2)}) async-start(f32[16,1,224]{2,1,0:T(1,128)} %broadcast_in_dim.42), calls=%async_computation.5 | async-start | bytes 32768 | tf_op jit(solution)/shard_map/all_to_all | solution.py:35
  460.6 21.0 %copy-start.7 = (bf16[4,224,224]{1,2,0:T(8,128)(2,1)S(1)}, bf16[4,224,224]{1,2,0:T(8,128)(2,1)}, u32[]{:S(2)}) copy-start(bf16[4,224,224]{1,2,0:T(8,128)(2,1)} %copy-done.6) | copy-start | bytes 1204228
  470.6 42.8 %all-to-all-start.11 = ((bf16[224,16,128]{2,0,1:T(8,128)(2,1)}), bf16[224,16,128]{2,0,1:T(8,128)(2,1)S(1)}, u32[]{:S(2)}, u32[]{:S(2)}) async-start(bf16[224,16,128]{2,0,1:T(8,128)(2,1)} %rev.9), calls=%async_computation.11 | async-start | bytes 1835008 | tf_op jit(solution)/shard_map/all_to_all | solution.py:57
  481.6 11.7 %copy-start.23 = (bf16[1,224,512]{2,1,0:T(8,128)(2,1)S(1)}, bf16[1,224,512]{2,1,0:T(8,128)(2,1)}, u32[]{:S(2)}) copy-start(bf16[1,224,512]{2,1,0:T(8,128)(2,1)} %param.8) | copy-start | bytes 688132
  482.9 10.3 %copy-start.17 = (f32[224,512]{1,0:T(8,128)S(1)}, f32[224,512]{1,0:T(8,128)}, u32[]{:S(2)}) copy-start(f32[224,512]{1,0:T(8,128)} %get-tuple-element.16) | copy-start | bytes 1376260
  485.3 23.9 %collective-permute-start.3 = (bf16[224,512]{1,0:T(8,128)(2,1)}, bf16[224,512]{1,0:T(8,128)(2,1)S(1)}, u32[]{:S(2)}, u32[]{:S(2)}) collective-permute-start(bf16[224,512]{1,0:T(8,128)(2,1)} %get-tuple-element.9), channel_id=1, source_target_pairs={{0,16},{16,32},{32,48},{48,64},{64,80},{80,96},{96,112},{112,128},... | collective-permute-start | bytes 688136 | tf_op jit(solution)/shard_map/ppermute | solution.py:45
  488.6 20.6 %collective-permute-start.1 = (bf16[224,512]{1,0:T(8,128)(2,1)}, bf16[224,512]{1,0:T(8,128)(2,1)}, u32[]{:S(2)}, u32[]{:S(2)}) collective-permute-start(bf16[224,512]{1,0:T(8,128)(2,1)} %get-tuple-element.10), channel_id=1, source_target_pairs={{16,0},{32,16},{48,32},{64,48},{80,64},{96,80},{112,96},{128,112},... | collective-permute-start | bytes 688136 | tf_op jit(solution)/shard_map/ppermute | solution.py:45
  493.5 16.6 %collective-permute-start.2 = (bf16[224,512]{1,0:T(8,128)(2,1)S(1)}, bf16[224,512]{1,0:T(8,128)(2,1)S(1)}, u32[]{:S(2)}, u32[]{:S(2)}) collective-permute-start(bf16[224,512]{1,0:T(8,128)(2,1)S(1)} %get-tuple-element.11), channel_id=1, source_target_pairs={{16,0},{32,16},{48,32},{64,48},{80,64},{96,80},{112,96},{128,112},... | collective-permute-start | bytes 688136 | tf_op jit(solution)/shard_map/ppermute | solution.py:45
  496.0 17.4 %copy-start.19 = (bf16[224,16,32]{0,2,1:T(8,128)(2,1)S(1)}, bf16[224,16,32]{0,2,1:T(8,128)(2,1)}, u32[]{:S(2)}) copy-start(bf16[224,16,32]{0,2,1:T(8,128)(2,1)} %copy-done.18) | copy-start | bytes 688132
  496.0 17.4 %collective-permute-start = (bf16[224,512]{1,0:T(8,128)(2,1)S(1)}, bf16[224,512]{1,0:T(8,128)(2,1)S(1)}, u32[]{:S(2)}, u32[]{:S(2)}) collective-permute-start(bf16[224,512]{1,0:T(8,128)(2,1)S(1)} %get-tuple-element.12), channel_id=1, source_target_pairs={{0,16},{16,32},{32,48},{48,64},{64,80},{80,96},{96,112},{112,128},... | collective-permute-start | bytes 688136 | tf_op jit(solution)/shard_map/ppermute | solution.py:45
where the time goes:
time: 524 us; the launch traced here: 522 us
  blocking collectives  241 us (46%)
  starting transfers between devices  106 us (20%)
  waiting for transfers between devices  92.6 us (18%)
  matrix products  39 us (7%)
  local copies, waits for them, and re-layouts  27.4 us (5%)
  other arithmetic  15.6 us (3%)
    all_gather x4, blocking collectives, combine_tensor(): return lax.all_gather(share, 'tensor', axis=1, tiled=True)  241 us
    all_to_all x4, waiting for transfers between devices, sum_at_owner(): tiles = lax.all_to_all(cut_along(x, dim, count), axis, 0, 0, tiled=True)  40.8 us
    all_to_all x4, waiting for transfers between devices, copy_for_each(): lax.all_to_all(jnp.broadcast_to(x[None], (count, *x.shape)), axis, 0, 0,...  33.6 us
    all_to_all x4, starting transfers between devices, copy_for_each(): lax.all_to_all(jnp.broadcast_to(x[None], (count, *x.shape)), axis, 0, 0,...  29.2 us
    all_to_all x4, starting transfers between devices, sum_at_owner(): tiles = lax.all_to_all(cut_along(x, dim, count), axis, 0, 0, tiled=True)  27.4 us
    all_to_all x2, starting transfers between devices, reflect_blocks(): lax.all_to_all(shortened(flipped), 'section', split_axis=1, concat_axis=1...  23.5 us
    ppermute x4, starting transfers between devices, passed_along(): return lax.ppermute(x, axis, pairs)  13.9 us
    ppermute x4, waiting for transfers between devices, passed_along(): return lax.ppermute(x, axis, pairs)  11 us
  transfers between devices with their start and end apart: 16, of which 10 were waited for; matrix products, arithmetic and copies ran while one was open for 13% of the time, Pallas kernels for 0%

commit v1 on v0

--- a/solution.py
+++ b/solution.py
@@ -9,6 +9,11 @@
 HEAD_DIM = 128
 EPS = 1e-05
 NEG_BIG = -1e30
+
+
+def swapped_in(array, mesh_axis, dim):
+    sent = jnp.stack([array] * lax.axis_size(mesh_axis))
+    return jnp.concatenate(lax.all_to_all(sent, mesh_axis, 0, 0), axis=dim)
 
 
 def cut_along(x, dim, count):
@@ -47,7 +52,7 @@
 
 def combine_tensor(partial_value):
     share = sum_at_owner(partial_value, "tensor", 1).astype(jnp.bfloat16)
-    return lax.all_gather(share, "tensor", axis=1, tiled=True)
+    return swapped_in(share, "tensor", 1)
 
 
 def reflect_blocks(parts):

time: 524 us -> 490 us (0.935)
  blocking collectives: 241 us -> 13 us
  waiting for transfers between devices: 92.6 us -> 281 us
  matrix products: 39 us -> 32.6 us
  starting transfers between devices: 106 us -> 112 us
  local copies, waits for them, and re-layouts: 27.4 us -> 33.1 us
    all_gather x4 -> x0, blocking collectives: 241 us -> none  [combine_tensor(): return lax.all_gather(share, 'tensor', axis=1, tiled=True)]
    all_to_all x4, waiting for transfers between devices: 40.8 us -> 149 us  [sum_at_owner(): tiles = lax.all_to_all(cut_along(x, dim, count), axis, 0, 0, tiled=True)]
    all_to_all x0 -> x4, waiting for transfers between devices: none -> 67.9 us  [swapped_in(): return jnp.concatenate(lax.all_to_all(sent, mesh_axis, 0, 0), axis=dim)]
    all_to_all x0 -> x4, starting transfers between devices: none -> 18.9 us  [swapped_in(): return jnp.concatenate(lax.all_to_all(sent, mesh_axis, 0, 0), axis=dim)]
    all_to_all x1, waiting for transfers between devices: 0.01 us -> 18.7 us  [mirror_terms(): lax.all_to_all(split[1], 'section', split_axis=1, concat_axis=1, tiled=True)]
    all_to_all x1, starting transfers between devices: 4.43 us -> 21.1 us  [mirror_terms(): lax.all_to_all(split[1], 'section', split_axis=1, concat_axis=1, tiled=True)]
    all_to_all x4 -> x3, starting transfers between devices: 29.2 us -> 16.2 us  [copy_for_each(): lax.all_to_all(jnp.broadcast_to(x[None], (count, *x.shape)), axis, 0, 0,...]
    all_to_all x0 -> x1, blocking collectives: none -> 13 us  [copy_for_each(): lax.all_to_all(jnp.broadcast_to(x[None], (count, *x.shape)), axis, 0, 0,...]
  transfers between devices with their start and end apart: 16 -> 19, of which waited for: 10 -> 17; matrix products, arithmetic and copies ran while one was open for 13% -> 13% of each run, Pallas kernels for 0% -> 0%
where the time goes in v1:
time: 490 us; the launch traced here: 487 us
  waiting for transfers between devices  281 us (57%)
  starting transfers between devices  112 us (23%)
  local copies, waits for them, and re-layouts  33.1 us (7%)
  matrix products  32.6 us (7%)
  other arithmetic  14.5 us (3%)
  blocking collectives  13 us (3%)
    all_to_all x4, waiting for transfers between devices, sum_at_owner(): tiles = lax.all_to_all(cut_along(x, dim, count), axis, 0, 0, tiled=True)  149 us
    all_to_all x4, waiting for transfers between devices, swapped_in(): return jnp.concatenate(lax.all_to_all(sent, mesh_axis, 0, 0), axis=dim)  67.9 us
    all_to_all x3, waiting for transfers between devices, copy_for_each(): lax.all_to_all(jnp.broadcast_to(x[None], (count, *x.shape)), axis, 0, 0,...  25.9 us
    all_to_all x1, starting transfers between devices, mirror_terms(): lax.all_to_all(split[1], 'section', split_axis=1, concat_axis=1, tiled=True)  21.1 us
    all_to_all x4, starting transfers between devices, swapped_in(): return jnp.concatenate(lax.all_to_all(sent, mesh_axis, 0, 0), axis=dim)  18.9 us
    all_to_all x1, waiting for transfers between devices, mirror_terms(): lax.all_to_all(split[1], 'section', split_axis=1, concat_axis=1, tiled=True)  18.7 us
    all_to_all x2, starting transfers between devices, reflect_blocks(): lax.all_to_all(shortened(flipped), 'section', split_axis=1, concat_axis=1...  18.4 us
    all_to_all x4, starting transfers between devices, sum_at_owner(): tiles = lax.all_to_all(cut_along(x, dim, count), axis, 0, 0, tiled=True)  16.5 us
  transfers between devices with their start and end apart: 19, of which 17 were waited for; matrix products, arithmetic and copies ran while one was open for 13% of the time, Pallas kernels for 0%

profile of v1, /device:TPU:64, one launch (start us, length us, event | category | flops | bytes accessed | tf_op | source)
XLA Modules:
  0.0 487.5 jit_solution(15942455178023011693)
XLA Ops:
  2.3 9.2 %all-to-all-start.3 = ((f32[16,1,224]{2,1,0:T(1,128)}), f32[16,1,224]{2,1,0:T(1,128)S(1)}, u32[]{:S(2)}, u32[]{:S(2)}) async-start(f32[16,1,224]{2,1,0:T(1,128)} %broadcast_in_dim.40), calls=%async_computation.3 | async-start | bytes 32768 | tf_op jit(solution)/shard_map/all_to_all | solution.py:40
  13.7 7.8 %all-to-all-done.3 = f32[16,1,224]{2,1,0:T(1,128)S(1)} async-done(((f32[16,1,224]{2,1,0:T(1,128)}), f32[16,1,224]{2,1,0:T(1,128)S(1)}, u32[]{:S(2)}, u32[]{:S(2)}) %all-to-all-start.3) | async-done | bytes 14368 | tf_op jit(solution)/shard_map/all_to_all | solution.py:40
  22.2 3.5 all-to-all-start
  26.5 9.1 %all-to-all-done = f32[16,1,224]{2,1,0:T(1,128)S(1)} async-done(((f32[16,1,224]{2,1,0:T(1,128)}), f32[16,1,224]{2,1,0:T(1,128)S(1)}, u32[]{:S(2)}, u32[]{:S(2)}) %all-to-all-start) | async-done | bytes 14368 | tf_op jit(solution)/shard_map/all_to_all | solution.py:40
  35.6 7.3 %all-to-all-start.12 = ((bf16[224,16,32]{0,2,1:T(8,128)(2,1)}), bf16[224,16,32]{0,2,1:T(8,128)(2,1)S(1)}, u32[]{:S(2)}, u32[]{:S(2)}) async-start(bf16[224,16,32]{0,2,1:T(8,128)(2,1)} %multiply_convert_fusion), calls=%async_computation.12 | async-start | bytes 524288 | tf_op jit(solution)/shard_map/all_to_all | solution.py:74
  42.9 2.9 copy.207
  45.8 2.1 convolution_bitcast_fusion
  47.9 4.2 all-to-all-done.12
  52.1 4.4 all-to-all-start.4
  56.5 2.9 copy.206
  60.1 2.0 convolution_bitcast_fusion.1
  62.1 42.9 %all-to-all-done.4 = f32[16,224,128]{2,1,0:T(8,128)} async-done(((f32[16,224,128]{2,1,0:T(8,128)}), f32[16,224,128]{2,1,0:T(8,128)}, u32[]{:S(2)}, u32[]{:S(2)}) %all-to-all-start.4) | async-done | bytes 1835040 | tf_op jit(solution)/shard_map/all_to_all | solution.py:26
  105.0 3.7 all-to-all-start.1
  110.4 38.4 %all-to-all-done.1 = f32[16,224,128]{2,1,0:T(8,128)S(1)} async-done(((f32[16,224,128]{2,1,0:T(8,128)}), f32[16,224,128]{2,1,0:T(8,128)S(1)}, u32[]{:S(2)}, u32[]{:S(2)}) %all-to-all-start.1) | async-done | bytes 1835040 | tf_op jit(solution)/shard_map/all_to_all | solution.py:26
  149.7 3.6 all-to-all-start.5
  160.3 12.1 %all-to-all-done.5 = bf16[16,224,128]{2,1,0:T(8,128)(2,1)S(1)} async-done(((bf16[16,224,128]{2,1,0:T(8,128)(2,1)}), bf16[16,224,128]{2,1,0:T(8,128)(2,1)S(1)}, u32[]{:S(2)}, u32[]{:S(2)}) %all-to-all-start.5) | async-done | bytes 917536 | tf_op jit(solution)/shard_map/all_to_all | solution.py:16
  172.3 13.3 %all-to-all-start.13 = ((bf16[224,16,32]{0,2,1:T(8,128)(2,1)}), bf16[224,16,32]{0,2,1:T(8,128)(2,1)S(1)}, u32[]{:S(2)}, u32[]{:S(2)}) async-start(bf16[224,16,32]{0,2,1:T(8,128)(2,1)} %rev.8), calls=%async_computation.13 | async-start | bytes 524288 | tf_op jit(solution)/shard_map/all_to_all | solution.py:62
  190.0 4.3 all-to-all-done.13
  195.3 4.0 all-to-all-start.2
  203.1 1.8 copy.197
  204.9 23.3 %all-to-all-done.2 = bf16[16,224,128]{2,1,0:T(8,128)(2,1)S(1)} async-done(((bf16[16,224,128]{2,1,0:T(8,128)(2,1)}), bf16[16,224,128]{2,1,0:T(8,128)(2,1)S(1)}, u32[]{:S(2)}, u32[]{:S(2)}) %all-to-all-start.2) | async-done | bytes 917536 | tf_op jit(solution)/shard_map/all_to_all | solution.py:16
  229.1 3.9 all-to-all-start.9
  235.6 2.6 fusion.109
  244.2 1.8 copy.186
  246.0 32.5 %all-to-all-done.9 = f32[16,224,128]{2,1,0:T(8,128)S(1)} async-done(((f32[16,224,128]{2,1,0:T(8,128)}), f32[16,224,128]{2,1,0:T(8,128)S(1)}, u32[]{:S(2)}, u32[]{:S(2)}) %all-to-all-start.9) | async-done | bytes 1835040 | tf_op jit(solution)/shard_map/all_to_all | solution.py:26
  278.5 4.4 all-to-all-start.6
  283.0 34.9 %all-to-all-done.6 = f32[16,224,128]{2,1,0:T(8,128)} async-done(((f32[16,224,128]{2,1,0:T(8,128)}), f32[16,224,128]{2,1,0:T(8,128)}, u32[]{:S(2)}, u32[]{:S(2)}) %all-to-all-start.6) | async-done | bytes 1835040 | tf_op jit(solution)/shard_map/all_to_all | solution.py:26
  319.0 7.6 %all-to-all-start.10 = ((bf16[16,224,128]{2,1,0:T(8,128)(2,1)}), bf16[16,224,128]{2,1,0:T(8,128)(2,1)}, u32[]{:S(2)}, u32[]{:S(2)}) async-start(bf16[16,224,128]{2,1,0:T(8,128)(2,1)} %stack.11), calls=%async_computation.10 | async-start | bytes 1835008 | tf_op jit(solution)/shard_map/all_to_all | solution.py:16
  328.2 17.5 %all-to-all-done.10 = bf16[16,224,128]{2,1,0:T(8,128)(2,1)} async-done(((bf16[16,224,128]{2,1,0:T(8,128)(2,1)}), bf16[16,224,128]{2,1,0:T(8,128)(2,1)}, u32[]{:S(2)}, u32[]{:S(2)}) %all-to-all-start.10) | async-done | bytes 917536 | tf_op jit(solution)/shard_map/all_to_all | solution.py:16
  346.8 3.6 all-to-all-start.7
  350.8 3.5 fusion.55
  354.3 15.2 %all-to-all-done.7 = bf16[16,224,128]{2,1,0:T(8,128)(2,1)S(1)} async-done(((bf16[16,224,128]{2,1,0:T(8,128)(2,1)}), bf16[16,224,128]{2,1,0:T(8,128)(2,1)S(1)}, u32[]{:S(2)}, u32[]{:S(2)}) %all-to-all-start.7) | async-done | bytes 917536 | tf_op jit(solution)/shard_map/all_to_all | solution.py:16
  369.5 13.0 %all_to_all.84 = f32[16,1,224]{2,1,0:T(1,128)S(1)} all-to-all(f32[16,1,224]{2,1,0:T(1,128)S(1)} %broadcast_in_dim.44), channel_id=1, replica_groups=mesh['section'=16,'tensor'=16] {'tensor'}, dimensions={0} | all-to-all | bytes 28672 | tf_op jit(solution)/shard_map/all_to_all | solution.py:40
  382.4 21.1 %all-to-all-start.14 = ((bf16[224,16,128]{2,0,1:T(8,128)(2,1)}), bf16[224,16,128]{2,0,1:T(8,128)(2,1)S(1)}, u32[]{:S(2)}, u32[]{:S(2)}) async-start(bf16[224,16,128]{2,0,1:T(8,128)(2,1)} %bitcast.43), calls=%async_computation.14 | async-start | bytes 1835008 | tf_op jit(solution)/shard_map/all_to_all | solution.py:75
  404.9 3.2 fusion.61
  408.1 18.7 %all-to-all-done.14 = bf16[224,16,128]{2,0,1:T(8,128)(2,1)S(1)} async-done(((bf16[224,16,128]{2,0,1:T(8,128)(2,1)}), bf16[224,16,128]{2,0,1:T(8,128)(2,1)S(1)}, u32[]{:S(2)}, u32[]{:S(2)}) %all-to-all-start.14) | async-done | bytes 917536 | tf_op jit(solution)/shard_map/all_to_all | solution.py:75
  427.4 3.5 all-to-all-start.8
  431.9 8.9 %all-to-all-done.8 = f32[16,1,224]{2,1,0:T(1,128)S(1)} async-done(((f32[16,1,224]{2,1,0:T(1,128)}), f32[16,1,224]{2,1,0:T(1,128)S(1)}, u32[]{:S(2)}, u32[]{:S(2)}) %all-to-all-start.8) | async-done | bytes 14368 | tf_op jit(solution)/shard_map/all_to_all | solution.py:40
  440.8 5.1 %all-to-all-start.15 = ((bf16[224,16,128]{2,0,1:T(8,128)(2,1)}), bf16[224,16,128]{2,0,1:T(8,128)(2,1)S(1)}, u32[]{:S(2)}, u32[]{:S(2)}) async-start(bf16[224,16,128]{2,0,1:T(8,128)(2,1)} %rev.9), calls=%async_computation.15 | async-start | bytes 1835008 | tf_op jit(solution)/shard_map/all_to_all | solution.py:62
  448.4 2.3 fusion.43
  450.7 3.4 collective-permute-start.3
  454.1 4.6 collective-permute-start.1
  459.0 2.5 collective-permute-start.2
  461.5 3.5 collective-permute-start
  465.0 2.8 fusion.34
  467.8 6.8 %collective-permute-done.3 = bf16[224,512]{1,0:T(8,128)(2,1)S(1)} collective-permute-done((bf16[224,512]{1,0:T(8,128)(2,1)}, bf16[224,512]{1,0:T(8,128)(2,1)S(1)}, u32[]{:S(2)}, u32[]{:S(2)}) %collective-permute-start.3) | collective-permute-done | bytes 229408 | tf_op jit(solution)/shard_map/ppermute | solution.py:50
  475.6 3.2 collective-permute-done
  478.9 4.9 %add_bitcast_fusion = f32[1,512,2048]{2,1,0:T(8,128)} fusion(f32[512,2048]{1,0:T(8,128)} %fusion.34, bf16[224,512]{0,1:T(8,128)(2,1)S(1)} %bitcast.230, bf16[224,16,128]{2,0,1:T(8,128)(2,1)S(1)} %all-to-all-done.15), kind=kOutput, calls=%fused_computation.4 | convolution fusion | flops 470810624 | bytes 9535488 | tf_op jit(solution)/shard_map/dot_general | solution.py:146
  (133 shorter events, 48.4 us)
Async XLA Ops:
  2.3 19.2 %all-to-all-start.3 = ((f32[16,1,224]{2,1,0:T(1,128)}), f32[16,1,224]{2,1,0:T(1,128)S(1)}, u32[]{:S(2)}, u32[]{:S(2)}) async-start(f32[16,1,224]{2,1,0:T(1,128)} %broadcast_in_dim.40), calls=%async_computation.3 | async-start | bytes 32768 | tf_op jit(solution)/shard_map/all_to_all | solution.py:40
  22.2 13.4 %all-to-all-start = ((f32[16,1,224]{2,1,0:T(1,128)}), f32[16,1,224]{2,1,0:T(1,128)S(1)}, u32[]{:S(2)}, u32[]{:S(2)}) async-start(f32[16,1,224]{2,1,0:T(1,128)} %broadcast_in_dim.36), calls=%async_computation | async-start | bytes 32768 | tf_op jit(solution)/shard_map/all_to_all | solution.py:40
  25.7 20.1 %copy-start.26 = (f32[224]{0:T(256)}, f32[224]{0:T(256)S(1)}, u32[]{:S(2)}) copy-start(f32[224]{0:T(256)S(1)} %add_rsqrt_fusion) | copy-start | bytes 2692
  35.6 16.5 %all-to-all-start.12 = ((bf16[224,16,32]{0,2,1:T(8,128)(2,1)}), bf16[224,16,32]{0,2,1:T(8,128)(2,1)S(1)}, u32[]{:S(2)}, u32[]{:S(2)}) async-start(bf16[224,16,32]{0,2,1:T(8,128)(2,1)} %multiply_convert_fusion), calls=%async_computation.12 | async-start | bytes 524288 | tf_op jit(solution)/shard_map/all_to_all | solution.py:74
  42.9 2.9 copy-start
  52.1 7.4 %copy-start.14 = (bf16[224,16,32]{0,2,1:T(8,128)(2,1)}, bf16[224,16,32]{0,2,1:T(8,128)(2,1)S(1)}, u32[]{:S(2)}) copy-start(bf16[224,16,32]{0,2,1:T(8,128)(2,1)S(1)} %all-to-all-done.12) | copy-start | bytes 688132
  52.1 52.9 %all-to-all-start.4 = ((f32[16,224,128]{2,1,0:T(8,128)}), f32[16,224,128]{2,1,0:T(8,128)}, u32[]{:S(2)}, u32[]{:S(2)}) async-start(f32[16,224,128]{2,1,0:T(8,128)} %convolution_bitcast_fusion), calls=%async_computation.4 | async-start | bytes 3670016 | tf_op jit(solution)/shard_map/all_to_all | solution.py:26
  56.5 3.6 copy-start.1
  105.0 43.7 %all-to-all-start.1 = ((f32[16,224,128]{2,1,0:T(8,128)}), f32[16,224,128]{2,1,0:T(8,128)S(1)}, u32[]{:S(2)}, u32[]{:S(2)}) async-start(f32[16,224,128]{2,1,0:T(8,128)} %convolution_bitcast_fusion.1), calls=%async_computation.1 | async-start | bytes 3670016 | tf_op jit(solution)/shard_map/all_to_all | solution.py:26
  149.7 22.6 %all-to-all-start.5 = ((bf16[16,224,128]{2,1,0:T(8,128)(2,1)}), bf16[16,224,128]{2,1,0:T(8,128)(2,1)S(1)}, u32[]{:S(2)}, u32[]{:S(2)}) async-start(bf16[16,224,128]{2,1,0:T(8,128)(2,1)} %stack.9), calls=%async_computation.5 | async-start | bytes 1835008 | tf_op jit(solution)/shard_map/all_to_all | solution.py:16
  172.3 21.9 %all-to-all-start.13 = ((bf16[224,16,32]{0,2,1:T(8,128)(2,1)}), bf16[224,16,32]{0,2,1:T(8,128)(2,1)S(1)}, u32[]{:S(2)}, u32[]{:S(2)}) async-start(bf16[224,16,32]{0,2,1:T(8,128)(2,1)} %rev.8), calls=%async_computation.13 | async-start | bytes 524288 | tf_op jit(solution)/shard_map/all_to_all | solution.py:62
  185.8 0.7 copy-start.22
  185.8 1.0 copy-start.11
  185.8 1.0 copy-start.27
  186.8 1.5 copy-start.17
  188.3 7.0 %copy-start.29 = (f32[4,224]{1,0:T(4,128)}, f32[4,224]{1,0:T(4,128)S(1)}, u32[]{:S(2)}) copy-start(f32[4,224]{1,0:T(4,128)S(1)} %get-tuple-element.17) | copy-start | bytes 10756
  188.3 11.0 %copy-start.3 = (bf16[224,4,128]{2,1,0:T(4,128)(2,1)S(1)}, bf16[224,4,128]{2,1,0:T(4,128)(2,1)}, u32[]{:S(2)}) copy-start(bf16[224,4,128]{2,1,0:T(4,128)(2,1)} %reshape.266) | copy-start | bytes 688132
  190.0 11.5 %copy-start.4 = (bf16[224,4,128]{2,1,0:T(4,128)(2,1)}, bf16[224,4,128]{2,1,0:T(4,128)(2,1)S(1)}, u32[]{:S(2)}) copy-start(bf16[224,4,128]{2,1,0:T(4,128)(2,1)S(1)} %convolution_bitcast_fusion.11) | copy-start | bytes 688132
  194.3 1.0 copy-start.12
  195.3 32.8 %all-to-all-start.2 = ((bf16[16,224,128]{2,1,0:T(8,128)(2,1)}), bf16[16,224,128]{2,1,0:T(8,128)(2,1)S(1)}, u32[]{:S(2)}, u32[]{:S(2)}) async-start(bf16[16,224,128]{2,1,0:T(8,128)(2,1)} %stack.8), calls=%async_computation.2 | async-start | bytes 1835008 | tf_op jit(solution)/shard_map/all_to_all | solution.py:16
  199.7 2.1 copy-start.23
  199.7 2.5 copy-start.28
  201.5 1.5 copy-start.7
  228.1 0.9 copy-start.2
  229.1 49.4 %all-to-all-start.9 = ((f32[16,224,128]{2,1,0:T(8,128)}), f32[16,224,128]{2,1,0:T(8,128)S(1)}, u32[]{:S(2)}, u32[]{:S(2)}) async-start(f32[16,224,128]{2,1,0:T(8,128)} %copy.197), calls=%async_computation.9 | async-start | bytes 3670016 | tf_op jit(solution)/shard_map/all_to_all | solution.py:26
  234.2 1.4 copy-start.25
  235.6 2.6 copy-start.19
  238.2 3.7 copy-start.15
  240.9 0.7 copy-start.6
  241.9 1.0 copy-start.10
  242.2 1.5 copy-start.9
  278.5 39.4 %all-to-all-start.6 = ((f32[16,224,128]{2,1,0:T(8,128)}), f32[16,224,128]{2,1,0:T(8,128)}, u32[]{:S(2)}, u32[]{:S(2)}) async-start(f32[16,224,128]{2,1,0:T(8,128)} %copy.186), calls=%async_computation.6 | async-start | bytes 3670016 | tf_op jit(solution)/shard_map/all_to_all | solution.py:26
  319.0 26.8 %all-to-all-start.10 = ((bf16[16,224,128]{2,1,0:T(8,128)(2,1)}), bf16[16,224,128]{2,1,0:T(8,128)(2,1)}, u32[]{:S(2)}, u32[]{:S(2)}) async-start(bf16[16,224,128]{2,1,0:T(8,128)(2,1)} %stack.11), calls=%async_computation.10 | async-start | bytes 1835008 | tf_op jit(solution)/shard_map/all_to_all | solution.py:16
  326.6 23.8 %copy-start.8 = (bf16[4,224,224]{1,2,0:T(8,128)(2,1)S(1)}, bf16[4,224,224]{1,2,0:T(8,128)(2,1)}, u32[]{:S(2)}) copy-start(bf16[4,224,224]{1,2,0:T(8,128)(2,1)} %copy-done.7) | copy-start | bytes 1204228
  326.6 23.8 %copy-start.18 = (bf16[224,4,128]{2,1,0:T(4,128)(2,1)S(1)}, bf16[224,4,128]{2,1,0:T(4,128)(2,1)}, u32[]{:S(2)}) copy-start(bf16[224,4,128]{2,1,0:T(4,128)(2,1)} %copy-done.17) | copy-start | bytes 688132
  346.8 22.7 %all-to-all-start.7 = ((bf16[16,224,128]{2,1,0:T(8,128)(2,1)}), bf16[16,224,128]{2,1,0:T(8,128)(2,1)S(1)}, u32[]{:S(2)}, u32[]{:S(2)}) async-start(bf16[16,224,128]{2,1,0:T(8,128)(2,1)} %stack.10), calls=%async_computation.7 | async-start | bytes 1835008 | tf_op jit(solution)/shard_map/all_to_all | solution.py:16
  350.8 52.7 %copy-start.20 = (bf16[224,4,128]{2,1,0:T(4,128)(2,1)S(1)}, bf16[224,4,128]{2,1,0:T(4,128)(2,1)}, u32[]{:S(2)}) copy-start(bf16[224,4,128]{2,1,0:T(4,128)(2,1)} %copy-done.19) | copy-start | bytes 688132
  382.4 44.3 %all-to-all-start.14 = ((bf16[224,16,128]{2,0,1:T(8,128)(2,1)}), bf16[224,16,128]{2,0,1:T(8,128)(2,1)S(1)}, u32[]{:S(2)}, u32[]{:S(2)}) async-start(bf16[224,16,128]{2,0,1:T(8,128)(2,1)} %bitcast.43), calls=%async_computation.14 | async-start | bytes 1835008 | tf_op jit(solution)/shard_map/all_to_all | solution.py:75
  408.1 37.8 %copy-start.5 = (bf16[224,4,128]{2,1,0:T(4,128)(2,1)S(1)}, bf16[224,4,128]{2,1,0:T(4,128)(2,1)}, u32[]{:S(2)}) copy-start(bf16[224,4,128]{2,1,0:T(4,128)(2,1)} %copy-done.4) | copy-start | bytes 688132
  427.4 13.4 %all-to-all-start.8 = ((f32[16,1,224]{2,1,0:T(1,128)}), f32[16,1,224]{2,1,0:T(1,128)S(1)}, u32[]{:S(2)}, u32[]{:S(2)}) async-start(f32[16,1,224]{2,1,0:T(1,128)} %broadcast_in_dim.42), calls=%async_computation.8 | async-start | bytes 32768 | tf_op jit(solution)/shard_map/all_to_all | solution.py:40
  440.8 38.1 %all-to-all-start.15 = ((bf16[224,16,128]{2,0,1:T(8,128)(2,1)}), bf16[224,16,128]{2,0,1:T(8,128)(2,1)S(1)}, u32[]{:S(2)}, u32[]{:S(2)}) async-start(bf16[224,16,128]{2,0,1:T(8,128)(2,1)} %rev.9), calls=%async_computation.15 | async-start | bytes 1835008 | tf_op jit(solution)/shard_map/all_to_all | solution.py:62
  447.1 11.7 %copy-start.16 = (bf16[1,224,512]{2,1,0:T(8,128)(2,1)S(1)}, bf16[1,224,512]{2,1,0:T(8,128)(2,1)}, u32[]{:S(2)}) copy-start(bf16[1,224,512]{2,1,0:T(8,128)(2,1)} %param.8) | copy-start | bytes 688132
  448.4 10.3 %copy-start.21 = (f32[224,512]{1,0:T(8,128)S(1)}, f32[224,512]{1,0:T(8,128)}, u32[]{:S(2)}) copy-start(f32[224,512]{1,0:T(8,128)} %get-tuple-element.16) | copy-start | bytes 1376260
  450.7 23.9 %collective-permute-start.3 = (bf16[224,512]{1,0:T(8,128)(2,1)}, bf16[224,512]{1,0:T(8,128)(2,1)S(1)}, u32[]{:S(2)}, u32[]{:S(2)}) collective-permute-start(bf16[224,512]{1,0:T(8,128)(2,1)} %get-tuple-element.9), channel_id=1, source_target_pairs={{0,16},{16,32},{32,48},{48,64},{64,80},{80,96},{96,112},{112,128},... | collective-permute-start | bytes 688136 | tf_op jit(solution)/shard_map/ppermute | solution.py:50
  454.1 20.6 %collective-permute-start.1 = (bf16[224,512]{1,0:T(8,128)(2,1)}, bf16[224,512]{1,0:T(8,128)(2,1)}, u32[]{:S(2)}, u32[]{:S(2)}) collective-permute-start(bf16[224,512]{1,0:T(8,128)(2,1)} %get-tuple-element.10), channel_id=1, source_target_pairs={{16,0},{32,16},{48,32},{64,48},{80,64},{96,80},{112,96},{128,112},... | collective-permute-start | bytes 688136 | tf_op jit(solution)/shard_map/ppermute | solution.py:50
  459.0 16.6 %collective-permute-start.2 = (bf16[224,512]{1,0:T(8,128)(2,1)S(1)}, bf16[224,512]{1,0:T(8,128)(2,1)S(1)}, u32[]{:S(2)}, u32[]{:S(2)}) collective-permute-start(bf16[224,512]{1,0:T(8,128)(2,1)S(1)} %get-tuple-element.11), channel_id=1, source_target_pairs={{16,0},{32,16},{48,32},{64,48},{80,64},{96,80},{112,96},{128,112},... | collective-permute-start | bytes 688136 | tf_op jit(solution)/shard_map/ppermute | solution.py:50
  461.4 17.4 %copy-start.13 = (bf16[224,16,32]{0,2,1:T(8,128)(2,1)S(1)}, bf16[224,16,32]{0,2,1:T(8,128)(2,1)}, u32[]{:S(2)}) copy-start(bf16[224,16,32]{0,2,1:T(8,128)(2,1)} %copy-done.12) | copy-start | bytes 688132
  461.5 17.4 %collective-permute-start = (bf16[224,512]{1,0:T(8,128)(2,1)S(1)}, bf16[224,512]{1,0:T(8,128)(2,1)S(1)}, u32[]{:S(2)}, u32[]{:S(2)}) collective-permute-start(bf16[224,512]{1,0:T(8,128)(2,1)S(1)} %get-tuple-element.12), channel_id=1, source_target_pairs={{0,16},{16,32},{32,48},{48,64},{64,80},{80,96},{96,112},{112,128},... | collective-permute-start | bytes 688136 | tf_op jit(solution)/shard_map/ppermute | solution.py:50
  (1 other events, 0.6 us)
